TPU v7x, 512 devices: a whole 4x8x8 slice. The times are simulated.
512 devices in a mesh: row: 32 (over z, x), col: 16 (over y, core).
Axes of the slice: x: 4, y: 8, z: 8, core: 2. Of those that a mesh axis runs over, the one named last changes fastest.
Arguments:
- tiles: bfloat16 [32, 16, 32, 128, 128], P('row', 'col'), may hold values from -0.375 to 0.375
- coords: int32 [32, 16, 32, 2], P('row', 'col'), may hold values from 0 to 2047, as said below
- counts: int32 [32, 16], P('row', 'col'), may hold values from 16 to 32, as said below
- rhs: float32 [2, 4194304], P(None, ('row', 'col')), may hold values from -50 to 50
Outputs:
- solution: float32 [2, 4194304], P(None, ('col', 'row'))
- phi_bar: float32 [2], replicated
Inputs may be any that keep to these rules, and one draw needn't show every extreme that they name: coords[p, q, k, 0] is a local block row below 1024 and coords[p, q, k, 1] a local block column below 2048; within one tile no two slots share a block row and no two share a block column; counting all 32 slots of a tile, exactly 2 of its block rows fall in each of the 16 ranges of 64 consecutive block rows, and exactly 1 of its block columns in each of the 32 ranges of 64 consecutive block columns. The first counts[p, q] slots of tile (p, q) are used; some tile uses all 32.
All inputs are finite; a program needn't handle non-finite values.
Results may differ from a plain program's by a relative error of at most 0.015.
Values may be sent and summed in bfloat16 or wider, within the bound.
No kernel may reach another device: no remote copies, remote signals or barrier semaphores. Data moves between devices by JAX's collectives and lax.ppermute only.
A program may use at most 192 MiB of HBM per device.

v0:
```python
import jax
import jax.numpy as jnp
from jax import lax
from jax.sharding import PartitionSpec as P

ITERS = 2
EPS = 1e-06


def rounded(values):
    return lax.optimization_barrier(values.astype(jnp.bfloat16))


def select_blocks(piece, block_ids, block):
    width = piece.shape[1]
    offsets = block_ids[:, None] * block + jnp.arange(block, dtype=jnp.int32)[None, :]
    inside = (offsets >= 0) & (offsets < width)
    clipped = jnp.clip(offsets, 0, width - 1)
    taken = jnp.take(piece, clipped.reshape(-1), axis=1).reshape(
        piece.shape[0], block_ids.shape[0], block
    )
    taken = jnp.where(inside[None, :, :], taken, jnp.zeros_like(taken))
    values = piece.astype(jnp.float32)
    return (taken, jnp.sum(values * values, axis=1))


def forward_products(picked, tile_data):
    return jnp.einsum("rkc,kdc->krd", picked, tile_data, preferred_element_type=jnp.float32)


def adjoint_products(picked, tile_data):
    return jnp.einsum("rkd,kdc->krc", picked, tile_data, preferred_element_type=jnp.float32)


def bucket_blocks(products, block_ids, valid, range_len, owners):
    slot_count = block_ids.shape[0]
    capacity = slot_count // owners
    values = rounded(products * valid[:, None, None])
    owner_ids = block_ids // range_len
    local_ids = block_ids % range_len
    slot_index = jnp.arange(slot_count, dtype=jnp.int32)
    live = valid > 0.5
    earlier = (
        (owner_ids[:, None] == owner_ids[None, :])
        & live[None, :]
        & (slot_index[None, :] < slot_index[:, None])
    )
    position = jnp.sum(earlier.astype(jnp.int32), axis=1)
    target = owner_ids * capacity + position
    onehot = (target[None, :] == jnp.arange(owners * capacity, dtype=jnp.int32)[:, None]) & live[
        None, :
    ]
    sent = jnp.einsum(
        "ek,krd->erd", onehot.astype(jnp.bfloat16), values, preferred_element_type=jnp.float32
    ).astype(jnp.bfloat16)
    sent = sent.reshape(owners, capacity, values.shape[1], values.shape[2])
    labels = jnp.sum(jnp.where(onehot, local_ids[None, :] + 1, 0), axis=1).reshape(owners, capacity)
    return (sent, labels)


def place_blocks(received, labels, range_len):
    flat = received.reshape(-1, received.shape[2], received.shape[3])
    flat_labels = labels.reshape(-1)
    placing = (
        flat_labels[None, :] == jnp.arange(1, range_len + 1, dtype=jnp.int32)[:, None]
    ).astype(jnp.bfloat16)
    summed = jnp.einsum("bk,krd->rbd", placing, flat, preferred_element_type=jnp.float32)
    return summed.reshape(flat.shape[1], range_len * flat.shape[2])


def on_device(tiles, coords, counts, rhs):
    tile_data = tiles[0, 0]
    row_ids = coords[0, 0, :, 0]
    col_ids = coords[0, 0, :, 1]
    slot_count = tile_data.shape[0]
    block = tile_data.shape[1]
    valid = (jnp.arange(slot_count, dtype=jnp.int32) < counts[0, 0]).astype(jnp.float32)
    realizations = rhs.shape[0]
    piece_len = rhs.shape[1]
    range_len = piece_len // block

    def fold_rows(piece):
        return select_blocks(piece, row_ids, block)

    def fold_cols(piece):
        return select_blocks(piece, col_ids, block)

    def gather_u(u_rounded):
        return fold_rows(lax.all_gather(u_rounded, "col", axis=1, tiled=True))

    def gather_v(v_rounded):
        return fold_cols(lax.all_gather(v_rounded, "row", axis=1, tiled=True))

    def own_norm(vector_bf):
        values = vector_bf.astype(jnp.float32)
        return jnp.sqrt(lax.psum(jnp.sum(values * values, axis=1), ("row", "col")) + EPS)

    def u_norm(u_rounded):
        return own_norm(u_rounded)

    def v_norm(v_piece):
        return own_norm(v_piece)

    def forward_sum(picked_v):
        products = forward_products(picked_v, tile_data)
        sent, labels = bucket_blocks(products, row_ids, valid, range_len, lax.axis_size("col"))
        received, got_labels = (
            lax.all_to_all(sent, "col", split_axis=0, concat_axis=0, tiled=True),
            lax.all_to_all(labels, "col", split_axis=0, concat_axis=0, tiled=True),
        )
        return place_blocks(received, got_labels, range_len)

    def adjoint(picked_u, beta_now, v_former):
        products = adjoint_products(picked_u, tile_data)
        sent, labels = bucket_blocks(products, col_ids, valid, range_len, lax.axis_size("row"))
        received, got_labels = (
            lax.all_to_all(sent, "row", split_axis=0, concat_axis=0, tiled=True),
            lax.all_to_all(labels, "row", split_axis=0, concat_axis=0, tiled=True),
        )
        summed = place_blocks(received, got_labels, range_len)
        v_rounded = rounded(summed / beta_now[:, None] - beta_now[:, None] * v_former)
        picked_v, squares = gather_v(v_rounded)
        return (v_rounded, v_rounded, picked_v, squares)

    u_rounded = rounded(rhs)
    picked_u, u_squares = gather_u(u_rounded)
    beta_now = u_norm(u_rounded)
    u_unit = u_rounded.astype(jnp.float32) / beta_now[:, None]
    v_store, v_piece, picked_v, v_squares = adjoint(picked_u, beta_now, jnp.zeros((), jnp.float32))
    alpha_now = v_norm(v_piece)
    v_unit = v_store.astype(jnp.float32) / alpha_now[:, None]
    direction = v_piece.astype(jnp.float32) / alpha_now[:, None]
    solution = jnp.zeros((realizations, piece_len), jnp.float32)
    phi_bar = beta_now
    rho_bar = alpha_now
    for step in range(ITERS):
        final_turn = step + 1 == ITERS
        summed = forward_sum(picked_v)
        u_rounded = rounded(summed / alpha_now[:, None] - alpha_now[:, None] * u_unit)
        if final_turn:
            beta_now = u_norm(u_rounded)
        else:
            picked_u, u_squares = gather_u(u_rounded)
            beta_now = u_norm(u_rounded)
        rho_value = jnp.sqrt(rho_bar * rho_bar + beta_now * beta_now)
        cosine = rho_bar / rho_value
        sine = beta_now / rho_value
        phi_value = cosine * phi_bar
        phi_bar = sine * phi_bar
        solution = solution + (phi_value / rho_value)[:, None] * direction
        u_unit = u_rounded.astype(jnp.float32) / beta_now[:, None]
        if not final_turn:
            v_store, v_piece, picked_v, v_squares = adjoint(picked_u, beta_now, v_unit)
            alpha_now = v_norm(v_piece)
            theta_value = sine * alpha_now
            rho_bar = -cosine * alpha_now
            v_unit = v_store.astype(jnp.float32) / alpha_now[:, None]
            piece_unit = v_piece.astype(jnp.float32) / alpha_now[:, None]
            direction = piece_unit - (theta_value / rho_value)[:, None] * direction
    return (solution, phi_bar)


def solution(mesh):
    return jax.shard_map(
        on_device,
        mesh=mesh,
        in_specs=(
            P("row", "col", None, None, None),
            P("row", "col", None, None),
            P("row", "col"),
            P(None, ("row", "col")),
        ),
        out_specs=(P(None, ("col", "row")), P()),
        check_vma=False,
    )
```

profile of v0, /device:TPU:1, one launch (start us, length us, event | category | flops | bytes accessed | tf_op | source)
XLA Modules:
  0.0 923.0 jit_solution(12879823360342886995)
XLA Ops:
  7.9 0.7 fusion.82
  8.6 0.8 bitcast_multiply_fusion.1
  9.4 0.7 and_select_fusion.1
  10.4 0.7 copy.71
  11.1 13.7 %all-to-all-start.1 = ((s32[32,1,1]{2,1,0:T(1,128)}), s32[32,1,1]{2,1,0:T(1,128)S(1)}, u32[]{:S(2)}, u32[]{:S(2)}) async-start(s32[32,1,1]{2,1,0:T(1,128)} %copy.71), calls=%async_computation.1 | async-start | bytes 32768 | tf_op jit(solution)/shard_map/all_to_all | solution.py:118
  25.0 0.9 convert_element_type.88
  25.9 19.8 %all_gather.12 = bf16[2,131072]{1,0:T(2,128)(2,1)S(1)} all-gather(bf16[2,8192]{1,0:T(2,128)(2,1)S(1)} %convert_element_type.88), channel_id=1, replica_groups=mesh['row'=32,'col'=16] {'col'}, dimensions={1}, use_global_device_ids=true | all-gather | bytes 557056 | tf_op jit(solution)/shard_map/all_gather | solution.py:89
  45.8 20.3 %copy.66 = bf16[2,131072]{0,1:T(8,128)(2,1)} copy(bf16[2,131072]{1,0:T(2,128)(2,1)S(1)} %all_gather.12) | data formatting | bytes 1048576 | tf_op jit(solution)/shard_map/all_gather | solution.py:89
  66.2 43.7 %gather_fusion = bf16[4096,2]{1,0:T(8,128)(2,1)S(1)} fusion(bf16[2,131072]{0,1:T(8,128)(2,1)} %copy.66, s32[4096]{0:T(1024)S(1)} %fusion.37), kind=kCustom, calls=%fused_computation.clone | custom fusion | bytes 49152 | tf_op jit(solution)/shard_map/jit(_take)/gather | solution.py:19
  109.8 2.1 broadcast_select_fusion.3
  112.8 97.2 %psum.35 = f32[2]{0:T(128)S(1)} all-reduce(f32[2]{0:T(128)S(1)} %fusion.13), channel_id=1, replica_groups=mesh['row'=32,'col'=16] {'row','col'}, use_global_device_ids=true, to_apply=%region_3.5 | all-reduce | flops 2 | bytes 16 | tf_op jit(solution)/shard_map/psum | solution.py:96
  210.2 0.6 copy.69
  210.8 5.6 all-to-all-start
  216.4 0.7 reduce
  217.1 7.8 all-to-all-done
  225.1 0.7 fusion.18
  225.9 0.7 all_to_all.30
  226.6 6.4 all-to-all-start.3
  233.1 6.9 all-to-all-done.3
  240.5 0.7 reduce.4
  241.2 0.9 fusion.14
  242.2 94.6 %psum.36 = f32[2]{0:T(128)S(1)} all-reduce(f32[2]{0:T(128)S(1)} %fusion.14), channel_id=1, replica_groups=mesh['row'=32,'col'=16] {'row','col'}, use_global_device_ids=true, to_apply=%region_5.7 | all-reduce | flops 2 | bytes 16 | tf_op jit(solution)/shard_map/psum | solution.py:96
  336.8 40.2 %copy.72 = bf16[2,262144]{0,1:T(8,128)(2,1)} copy(bf16[2,262144]{1,0:T(2,128)(2,1)} %all-gather.3.cloned.1.call-done) | data formatting | bytes 2097152 | tf_op jit(solution)/shard_map/all_gather | solution.py:92
  377.0 43.7 %gather_fusion.1 = bf16[4096,2]{1,0:T(8,128)(2,1)S(1)} fusion(bf16[2,262144]{0,1:T(8,128)(2,1)} %copy.72, s32[4096]{0:T(1024)S(1)} %fusion.32), kind=kCustom, calls=%fused_computation.1.clone | custom fusion | bytes 49152 | tf_op jit(solution)/shard_map/jit(_take)/gather | solution.py:19
  420.7 2.1 broadcast_select_fusion.1
  423.2 0.7 fusion.1
  424.0 0.6 copy.75
  424.6 4.1 all-to-all-start.2
  428.7 7.3 all-to-all-done.2
  436.4 16.5 %all_gather.14 = bf16[2,131072]{1,0:T(2,128)(2,1)S(1)} all-gather(bf16[2,8192]{1,0:T(2,128)(2,1)S(1)} %fusion.19), channel_id=1, replica_groups=mesh['row'=32,'col'=16] {'col'}, dimensions={1}, use_global_device_ids=true | all-gather | bytes 557056 | tf_op jit(solution)/shard_map/all_gather | solution.py:89
  453.1 20.3 %copy.78 = bf16[2,131072]{0,1:T(8,128)(2,1)} copy(bf16[2,131072]{1,0:T(2,128)(2,1)S(1)} %all_gather.14) | data formatting | bytes 1048576 | tf_op jit(solution)/shard_map/all_gather | solution.py:89
  473.4 43.7 %gather_fusion.2 = bf16[4096,2]{1,0:T(8,128)(2,1)S(1)} fusion(bf16[2,131072]{0,1:T(8,128)(2,1)} %copy.78, s32[4096]{0:T(1024)S(1)} %fusion.37), kind=kCustom, calls=%fused_computation.2.clone | custom fusion | bytes 49152 | tf_op jit(solution)/shard_map/jit(_take)/gather | solution.py:19
  517.1 2.1 broadcast_select_fusion.2
  520.2 0.6 copy.81
  520.8 4.8 all-to-all-start.4
  525.7 97.1 %psum.37 = f32[2]{0:T(128)S(1)} all-reduce(f32[2]{0:T(128)S(1)} %fusion.15), channel_id=1, replica_groups=mesh['row'=32,'col'=16] {'row','col'}, use_global_device_ids=true, to_apply=%region_9.12 | all-reduce | flops 2 | bytes 16 | tf_op jit(solution)/shard_map/psum | solution.py:96
  623.1 0.7 fusion.21
  623.9 1.0 fusion.16
  624.8 94.9 %psum.38 = f32[2]{0:T(128)S(1)} all-reduce(f32[2]{0:T(128)S(1)} %fusion.16), channel_id=1, replica_groups=mesh['row'=32,'col'=16] {'row','col'}, use_global_device_ids=true, to_apply=%region_11.14 | all-reduce | flops 2 | bytes 16 | tf_op jit(solution)/shard_map/psum | solution.py:96
  719.7 40.2 %copy.83 = bf16[2,262144]{0,1:T(8,128)(2,1)} copy(bf16[2,262144]{1,0:T(2,128)(2,1)} %all-gather.5.cloned.1.call-done) | data formatting | bytes 2097152 | tf_op jit(solution)/shard_map/all_gather | solution.py:92
  759.9 43.7 %gather_fusion.3 = bf16[4096,2]{1,0:T(8,128)(2,1)S(1)} fusion(bf16[2,262144]{0,1:T(8,128)(2,1)} %copy.83, s32[4096]{0:T(1024)S(1)} %fusion.32), kind=kCustom, calls=%fused_computation.3.clone | custom fusion | bytes 49152 | tf_op jit(solution)/shard_map/jit(_take)/gather | solution.py:19
  803.6 2.1 broadcast_select_fusion
  806.1 0.7 fusion.3
  806.9 0.6 copy.86
  807.5 4.4 all-to-all-start.5
  811.9 7.3 all-to-all-done.5
  819.8 95.0 %psum.39 = f32[2]{0:T(128)S(1)} all-reduce(f32[2]{0:T(128)S(1)} %multiply_reduce_fusion), channel_id=1, replica_groups=mesh['row'=32,'col'=16] {'row','col'}, use_global_device_ids=true, to_apply=%region_13.16 | all-reduce | flops 2 | bytes 16 | tf_op jit(solution)/shard_map/psum | solution.py:96
  915.4 0.8 multiply_add_fusion
  (54 shorter events, 6.8 us)
Async XLA Ops:
  7.2 105.3 %copy-start = (bf16[1,1,32,128,128]{4,3,2,1,0:T(8,128)(2,1)S(1)}, bf16[1,1,32,128,128]{4,3,2,1,0:T(8,128)(2,1)}, u32[]{:S(2)}) copy-start(bf16[1,1,32,128,128]{4,3,2,1,0:T(8,128)(2,1)} %param.8) | copy-start | bytes 3145732
  11.1 199.7 %all-to-all-start.1 = ((s32[32,1,1]{2,1,0:T(1,128)}), s32[32,1,1]{2,1,0:T(1,128)S(1)}, u32[]{:S(2)}, u32[]{:S(2)}) async-start(s32[32,1,1]{2,1,0:T(1,128)} %copy.71), calls=%async_computation.1 | async-start | bytes 32768 | tf_op jit(solution)/shard_map/all_to_all | solution.py:118
  210.8 14.1 %all-to-all-start = ((bf16[32,1,2,128]{3,2,1,0:T(2,128)(2,1)}), bf16[32,1,2,128]{3,2,1,0:T(2,128)(2,1)S(1)}, u32[]{:S(2)}, u32[]{:S(2)}) async-start(bf16[32,1,2,128]{3,2,1,0:T(2,128)(2,1)} %copy.69), calls=%async_computation | async-start | bytes 32768 | tf_op jit(solution)/shard_map/all_to_all | solution.py:117
  216.4 120.5 %all-gather.3.cloned.1.call-start = ((), (), s32[]{:S(2)}) async-start(), calls=%async_computation.6 | async-start | bytes 1081344 | tf_op jit(solution)/shard_map/all_gather | solution.py:92
  225.9 397.2 %copy-start.1 = (bf16[2,8192]{1,0:T(2,128)(2,1)S(1)}, bf16[2,8192]{1,0:T(2,128)(2,1)}, u32[]{:S(2)}) copy-start(bf16[2,8192]{1,0:T(2,128)(2,1)} %fusion.18) | copy-start | bytes 98308
  226.6 13.4 %all-to-all-start.3 = ((s32[16,1,2]{2,1,0:T(1,128)}), s32[16,1,2]{2,1,0:T(1,128)S(1)}, u32[]{:S(2)}, u32[]{:S(2)}) async-start(s32[16,1,2]{2,1,0:T(1,128)} %bitcast.19), calls=%async_computation.3 | async-start | bytes 16384 | tf_op jit(solution)/shard_map/all_to_all | solution.py:109
  424.6 11.4 %all-to-all-start.2 = ((bf16[16,2,2,128]{3,1,2,0:T(2,128)(2,1)}), bf16[16,2,2,128]{3,1,2,0:T(2,128)(2,1)S(1)}, u32[]{:S(2)}, u32[]{:S(2)}) async-start(bf16[16,2,2,128]{3,1,2,0:T(2,128)(2,1)} %copy.75), calls=%async_computation.2 | async-start | bytes 32768 | tf_op jit(solution)/shard_map/all_to_all | solution.py:108
  520.8 102.0 %all-to-all-start.4 = ((bf16[32,1,2,128]{3,2,1,0:T(2,128)(2,1)}), bf16[32,1,2,128]{3,2,1,0:T(2,128)(2,1)S(1)}, u32[]{:S(2)}, u32[]{:S(2)}) async-start(bf16[32,1,2,128]{3,2,1,0:T(2,128)(2,1)} %copy.81), calls=%async_computation.4 | async-start | bytes 32768 | tf_op jit(solution)/shard_map/all_to_all | solution.py:117
  525.6 194.1 %all-gather.5.cloned.1.call-start = ((), (), s32[]{:S(2)}) async-start(), calls=%async_computation.7 | async-start | bytes 1081344 | tf_op jit(solution)/shard_map/all_gather | solution.py:92
  623.8 291.5 %copy-start.2 = (bf16[2,8192]{1,0:T(2,128)(2,1)S(1)}, bf16[2,8192]{1,0:T(2,128)(2,1)}, u32[]{:S(2)}) copy-start(bf16[2,8192]{1,0:T(2,128)(2,1)} %get-tuple-element.20) | copy-start | bytes 98308
  807.5 11.7 %all-to-all-start.5 = ((bf16[16,2,2,128]{3,1,2,0:T(2,128)(2,1)}), bf16[16,2,2,128]{3,1,2,0:T(2,128)(2,1)S(1)}, u32[]{:S(2)}, u32[]{:S(2)}) async-start(bf16[16,2,2,128]{3,1,2,0:T(2,128)(2,1)} %copy.86), calls=%async_computation.5 | async-start | bytes 32768 | tf_op jit(solution)/shard_map/all_to_all | solution.py:108
Sparse Core Ops, SparseCore 0:
  226.0 71.4 all-gather.2
  624.0 71.4 all-gather.4
where the time goes:
time: 929 us; the launch traced here: 923 us
  blocking collectives  515 us (55%)
  local copies, waits for them, and re-layouts  302 us (33%)
  starting transfers between devices  39 us (4%)
  waiting for transfers between devices  29.3 us (3%)
  other arithmetic  19.2 us (2%)
  between operations  15 us (2%)
    psum x5, blocking collectives, own_norm(): lax.psum(jnp.sum(values * values, axis=1), ('row', 'col')) + EPS  479 us
    gather x4, local copies, waits for them, and re-layouts, select_blocks(): jnp.take(piece, clipped.reshape(-1), axis=1)  175 us
    all_gather x2, local copies, waits for them, and re-layouts, gather_v(): return fold_cols(lax.all_gather(v_rounded, 'row', axis=1, tiled=True))  80.3 us
    all_gather x2, local copies, waits for them, and re-layouts, gather_u(): return fold_rows(lax.all_gather(u_rounded, 'col', axis=1, tiled=True))  40.6 us
    all_gather x2, blocking collectives, gather_u(): return fold_rows(lax.all_gather(u_rounded, 'col', axis=1, tiled=True))  36.3 us
  transfers between devices with their start and end apart: 8, of which 4 were waited for; matrix products, arithmetic and copies ran while one was open for 8% of the time, Pallas kernels for 0%

commit v1 on v0

--- a/solution.py
+++ b/solution.py
@@ -89,7 +89,11 @@
         return fold_rows(lax.all_gather(u_rounded, "col", axis=1, tiled=True))
 
     def gather_v(v_rounded):
-        return fold_cols(lax.all_gather(v_rounded, "row", axis=1, tiled=True))
+        return fold_cols(
+            jnp.concatenate(
+                lax.all_to_all(jnp.stack([v_rounded] * lax.axis_size("row")), "row", 0, 0), axis=1
+            )
+        )
 
     def own_norm(vector_bf):
         values = vector_bf.astype(jnp.float32)

time: 929 us -> 960 us (1.033)
  blocking collectives: 515 us -> 551 us
  between operations: 15 us -> 1.64 us
  starting transfers between devices: 39 us -> 51.1 us
    all_gather x2 -> x0, local copies, waits for them, and re-layouts: 80.3 us -> none  [gather_v(): return fold_cols(lax.all_gather(v_rounded, 'row', axis=1, tiled=True))]
    reshape x0 -> x2, local copies, waits for them, and re-layouts: none -> 80.3 us  [gather_v(): jnp.concatenate(lax.all_to_all(jnp.stack([v_rounded] * lax.axis_size('row...]
    psum x5, blocking collectives: 479 us -> 515 us  [own_norm(): lax.psum(jnp.sum(values * values, axis=1), ('row', 'col')) + EPS]
    all_to_all x0 -> x2, starting transfers between devices: none -> 9.65 us  [gather_v(): lax.all_to_all(jnp.stack([v_rounded] * lax.axis_size('row')), 'row', 0, 0)]
  transfers between devices with their start and end apart: 8 -> 8, of which waited for: 4 -> 4; matrix products, arithmetic and copies ran while one was open for 8% -> 7% of each run, Pallas kernels for 0% -> 0%
where the time goes in v1:
time: 960 us; the launch traced here: 958 us
  blocking collectives  551 us (57%)
  local copies, waits for them, and re-layouts  305 us (32%)
  starting transfers between devices  51.1 us (5%)
  waiting for transfers between devices  28.6 us (3%)
  other arithmetic  16.4 us (2%)
    psum x5, blocking collectives, own_norm(): lax.psum(jnp.sum(values * values, axis=1), ('row', 'col')) + EPS  515 us
    gather x4, local copies, waits for them, and re-layouts, select_blocks(): jnp.take(piece, clipped.reshape(-1), axis=1)  175 us
    reshape x2, local copies, waits for them, and re-layouts, gather_v(): jnp.concatenate(lax.all_to_all(jnp.stack([v_rounded] * lax.axis_size('row...  80.3 us
    all_gather x2, local copies, waits for them, and re-layouts, gather_u(): return fold_rows(lax.all_gather(u_rounded, 'col', axis=1, tiled=True))  40.6 us
    all_gather x2, blocking collectives, gather_u(): return fold_rows(lax.all_gather(u_rounded, 'col', axis=1, tiled=True))  36.3 us
  transfers between devices with their start and end apart: 8, of which 4 were waited for; matrix products, arithmetic and copies ran while one was open for 7% of the time, Pallas kernels for 0%

profile of v1, /device:TPU:1, one launch (start us, length us, event | category | flops | bytes accessed | tf_op | source)
XLA Modules:
  0.0 957.8 jit_solution(5591673812600939221)
XLA Ops:
  1.4 0.7 fusion.82
  2.1 0.8 bitcast_multiply_fusion.1
  2.9 0.7 and_select_fusion.1
  3.9 0.7 copy.79
  4.6 13.7 %all-to-all-start.1 = ((s32[32,1,1]{2,1,0:T(1,128)}), s32[32,1,1]{2,1,0:T(1,128)S(1)}, u32[]{:S(2)}, u32[]{:S(2)}) async-start(s32[32,1,1]{2,1,0:T(1,128)} %copy.79), calls=%async_computation.1 | async-start | bytes 32768 | tf_op jit(solution)/shard_map/all_to_all | solution.py:122
  18.4 0.9 convert_element_type.88
  19.3 19.8 %all_gather.6 = bf16[2,131072]{1,0:T(2,128)(2,1)S(1)} all-gather(bf16[2,8192]{1,0:T(2,128)(2,1)S(1)} %convert_element_type.88), channel_id=1, replica_groups=mesh['row'=32,'col'=16] {'col'}, dimensions={1}, use_global_device_ids=true | all-gather | bytes 557056 | tf_op jit(solution)/shard_map/all_gather | solution.py:89
  39.3 20.3 %copy.74 = bf16[2,131072]{0,1:T(8,128)(2,1)} copy(bf16[2,131072]{1,0:T(2,128)(2,1)S(1)} %all_gather.6) | data formatting | bytes 1048576 | tf_op jit(solution)/shard_map/all_gather | solution.py:89
  59.6 43.7 %gather_fusion = bf16[4096,2]{1,0:T(8,128)(2,1)S(1)} fusion(bf16[2,131072]{0,1:T(8,128)(2,1)} %copy.74, s32[4096]{0:T(1024)S(1)} %fusion.37), kind=kCustom, calls=%fused_computation.clone | custom fusion | bytes 49152 | tf_op jit(solution)/shard_map/jit(_take)/gather | solution.py:19
  103.3 2.1 broadcast_select_fusion.3
  106.3 97.2 %psum.35 = f32[2]{0:T(128)S(1)} all-reduce(f32[2]{0:T(128)S(1)} %fusion.13), channel_id=1, replica_groups=mesh['row'=32,'col'=16] {'row','col'}, use_global_device_ids=true, to_apply=%region_3.5 | all-reduce | flops 2 | bytes 16 | tf_op jit(solution)/shard_map/psum | solution.py:100
  203.6 0.6 copy.77
  204.2 5.6 all-to-all-start
  209.8 0.7 all_to_all.37
  210.5 0.7 reduce
  211.2 7.2 all-to-all-done
  218.3 6.4 all-to-all-start.4
  225.1 6.6 all-to-all-done.4
  231.7 1.9 stack.4
  233.7 3.9 all-to-all-start.2
  238.3 0.7 reduce.4
  239.2 111.7 %psum.36 = f32[2]{0:T(128)S(1)} all-reduce(f32[2]{0:T(128)S(1)} %fusion.14), channel_id=1, replica_groups=mesh['row'=32,'col'=16] {'row','col'}, use_global_device_ids=true, to_apply=%region_5.7 | all-reduce | flops 2 | bytes 16 | tf_op jit(solution)/shard_map/psum | solution.py:100
  350.9 40.2 %copy.80 = bf16[2,32,8192]{0,2,1:T(8,128)(2,1)} copy(bf16[2,32,8192]{2,0,1:T(2,128)(2,1)S(1)} %bitcast.143) | data formatting | bytes 2097152 | tf_op jit(solution)/shard_map/reshape | solution.py:93
  391.1 43.7 %gather_fusion.1 = bf16[4096,2]{1,0:T(8,128)(2,1)S(1)} fusion(bf16[2,262144]{0,1:T(8,128)(2,1)} %bitcast.16, s32[4096]{0:T(1024)S(1)} %fusion.32), kind=kCustom, calls=%fused_computation.1.clone | custom fusion | bytes 49152 | tf_op jit(solution)/shard_map/jit(_take)/gather | solution.py:19
  434.8 2.1 broadcast_select_fusion.1
  437.3 0.7 fusion.1
  438.1 0.6 copy.83
  438.7 4.3 all-to-all-start.3
  443.0 7.4 all-to-all-done.3
  450.9 16.5 %all_gather.7 = bf16[2,131072]{1,0:T(2,128)(2,1)S(1)} all-gather(bf16[2,8192]{1,0:T(2,128)(2,1)S(1)} %fusion.19), channel_id=1, replica_groups=mesh['row'=32,'col'=16] {'col'}, dimensions={1}, use_global_device_ids=true | all-gather | bytes 557056 | tf_op jit(solution)/shard_map/all_gather | solution.py:89
  467.5 20.3 %copy.86 = bf16[2,131072]{0,1:T(8,128)(2,1)} copy(bf16[2,131072]{1,0:T(2,128)(2,1)S(1)} %all_gather.7) | data formatting | bytes 1048576 | tf_op jit(solution)/shard_map/all_gather | solution.py:89
  487.9 43.7 %gather_fusion.2 = bf16[4096,2]{1,0:T(8,128)(2,1)S(1)} fusion(bf16[2,131072]{0,1:T(8,128)(2,1)} %copy.86, s32[4096]{0:T(1024)S(1)} %fusion.37), kind=kCustom, calls=%fused_computation.2.clone | custom fusion | bytes 49152 | tf_op jit(solution)/shard_map/jit(_take)/gather | solution.py:19
  531.5 2.1 broadcast_select_fusion.2
  534.6 0.6 copy.89
  535.2 7.5 all-to-all-start.5
  542.8 97.1 %psum.37 = f32[2]{0:T(128)S(1)} all-reduce(f32[2]{0:T(128)S(1)} %fusion.15), channel_id=1, replica_groups=mesh['row'=32,'col'=16] {'row','col'}, use_global_device_ids=true, to_apply=%region_9.12 | all-reduce | flops 2 | bytes 16 | tf_op jit(solution)/shard_map/psum | solution.py:100
  640.3 1.9 stack.5
  642.2 5.7 all-to-all-start.6
  648.2 113.2 %psum.38 = f32[2]{0:T(128)S(1)} all-reduce(f32[2]{0:T(128)S(1)} %fusion.16), channel_id=1, replica_groups=mesh['row'=32,'col'=16] {'row','col'}, use_global_device_ids=true, to_apply=%region_11.14 | all-reduce | flops 2 | bytes 16 | tf_op jit(solution)/shard_map/psum | solution.py:100
  761.4 40.2 %copy.91 = bf16[2,32,8192]{0,2,1:T(8,128)(2,1)} copy(bf16[2,32,8192]{2,0,1:T(2,128)(2,1)S(1)} %bitcast.144) | data formatting | bytes 2097152 | tf_op jit(solution)/shard_map/reshape | solution.py:93
  801.6 43.7 %gather_fusion.3 = bf16[4096,2]{1,0:T(8,128)(2,1)S(1)} fusion(bf16[2,262144]{0,1:T(8,128)(2,1)} %bitcast.30, s32[4096]{0:T(1024)S(1)} %fusion.32), kind=kCustom, calls=%fused_computation.3.clone | custom fusion | bytes 49152 | tf_op jit(solution)/shard_map/jit(_take)/gather | solution.py:19
  845.2 2.1 broadcast_select_fusion
  847.8 0.7 fusion.3
  848.6 0.6 copy.94
  849.2 4.0 all-to-all-start.7
  853.2 7.4 all-to-all-done.7
  861.2 95.3 %psum.39 = f32[2]{0:T(128)S(1)} all-reduce(f32[2]{0:T(128)S(1)} %multiply_reduce_fusion), channel_id=1, replica_groups=mesh['row'=32,'col'=16] {'row','col'}, use_global_device_ids=true, to_apply=%region_13.16 | all-reduce | flops 2 | bytes 16 | tf_op jit(solution)/shard_map/psum | solution.py:100
  957.1 0.8 multiply_add_fusion
  (50 shorter events, 7.3 us)
Async XLA Ops:
  0.6 105.3 %copy-start = (bf16[1,1,32,128,128]{4,3,2,1,0:T(8,128)(2,1)S(1)}, bf16[1,1,32,128,128]{4,3,2,1,0:T(8,128)(2,1)}, u32[]{:S(2)}) copy-start(bf16[1,1,32,128,128]{4,3,2,1,0:T(8,128)(2,1)} %param.8) | copy-start | bytes 3145732
  4.6 199.7 %all-to-all-start.1 = ((s32[32,1,1]{2,1,0:T(1,128)}), s32[32,1,1]{2,1,0:T(1,128)S(1)}, u32[]{:S(2)}, u32[]{:S(2)}) async-start(s32[32,1,1]{2,1,0:T(1,128)} %copy.79), calls=%async_computation.1 | async-start | bytes 32768 | tf_op jit(solution)/shard_map/all_to_all | solution.py:122
  204.2 14.1 %all-to-all-start = ((bf16[32,1,2,128]{3,2,1,0:T(2,128)(2,1)}), bf16[32,1,2,128]{3,2,1,0:T(2,128)(2,1)S(1)}, u32[]{:S(2)}, u32[]{:S(2)}) async-start(bf16[32,1,2,128]{3,2,1,0:T(2,128)(2,1)} %copy.77), calls=%async_computation | async-start | bytes 32768 | tf_op jit(solution)/shard_map/all_to_all | solution.py:121
  218.3 13.4 %all-to-all-start.4 = ((s32[16,1,2]{2,1,0:T(1,128)}), s32[16,1,2]{2,1,0:T(1,128)S(1)}, u32[]{:S(2)}, u32[]{:S(2)}) async-start(s32[16,1,2]{2,1,0:T(1,128)} %bitcast.21), calls=%async_computation.4 | async-start | bytes 16384 | tf_op jit(solution)/shard_map/all_to_all | solution.py:113
  233.7 117.3 %all-to-all-start.2 = ((bf16[32,2,8192]{2,1,0:T(2,128)(2,1)}), bf16[32,2,8192]{2,1,0:T(2,128)(2,1)S(1)}, u32[]{:S(2)}, u32[]{:S(2)}) async-start(bf16[32,2,8192]{2,1,0:T(2,128)(2,1)} %stack.4), calls=%async_computation.2 | async-start | bytes 2097152 | tf_op jit(solution)/shard_map/all_to_all | solution.py:94
  438.7 11.7 %all-to-all-start.3 = ((bf16[16,2,2,128]{3,1,2,0:T(2,128)(2,1)}), bf16[16,2,2,128]{3,1,2,0:T(2,128)(2,1)S(1)}, u32[]{:S(2)}, u32[]{:S(2)}) async-start(bf16[16,2,2,128]{3,1,2,0:T(2,128)(2,1)} %copy.83), calls=%async_computation.3 | async-start | bytes 32768 | tf_op jit(solution)/shard_map/all_to_all | solution.py:112
  535.2 104.7 %all-to-all-start.5 = ((bf16[32,1,2,128]{3,2,1,0:T(2,128)(2,1)}), bf16[32,1,2,128]{3,2,1,0:T(2,128)(2,1)S(1)}, u32[]{:S(2)}, u32[]{:S(2)}) async-start(bf16[32,1,2,128]{3,2,1,0:T(2,128)(2,1)} %copy.89), calls=%async_computation.5 | async-start | bytes 32768 | tf_op jit(solution)/shard_map/all_to_all | solution.py:121
  642.2 119.1 %all-to-all-start.6 = ((bf16[32,2,8192]{2,1,0:T(2,128)(2,1)}), bf16[32,2,8192]{2,1,0:T(2,128)(2,1)S(1)}, u32[]{:S(2)}, u32[]{:S(2)}) async-start(bf16[32,2,8192]{2,1,0:T(2,128)(2,1)} %stack.5), calls=%async_computation.6 | async-start | bytes 2097152 | tf_op jit(solution)/shard_map/all_to_all | solution.py:94
  849.2 11.4 %all-to-all-start.7 = ((bf16[16,2,2,128]{3,1,2,0:T(2,128)(2,1)}), bf16[16,2,2,128]{3,1,2,0:T(2,128)(2,1)S(1)}, u32[]{:S(2)}, u32[]{:S(2)}) async-start(bf16[16,2,2,128]{3,1,2,0:T(2,128)(2,1)} %copy.94), calls=%async_computation.7 | async-start | bytes 32768 | tf_op jit(solution)/shard_map/all_to_all | solution.py:112
